TPU v7x, 32 devices: a whole 2x2x4 slice. The times are simulated.
32 devices in a mesh: groups: 2 (over y), pix: 8 (over z, x), dp: 2 (over core).
Axes of the slice: x: 2, y: 2, z: 4, core: 2. Of those that a mesh axis runs over, the one named last changes fastest.
Arguments:
- features: bfloat16 [64, 64, 512], P('pix', None, ('groups', 'dp')), parts along dimension 2, may hold values from -6 to 6
- cheb_weights: bfloat16 [4, 64, 64], replicated, may hold values from -0.375 to 0.375
- out_bias: float32 [64], replicated, may hold values from -3 to 3
- lap_tiles: bfloat16 [64, 64, 576], P('pix'), as said below
- neighbours: int32 [64, 2], P('pix'), may hold values from 0 to 15, as said below
- send_blocks: int32 [8, 4, 2], P('pix'), may hold values from 0 to 7, as said below
- pixel_mask: int32 [64, 64], P('pix'), may hold values 0 or 1
- cotangent: bfloat16 [64, 64, 512], P('pix', None, ('groups', 'dp')), parts along dimension 2, may hold values from -6 to 6
Outputs:
- output_maps: bfloat16 [64, 64, 512], P('pix', None, ('groups', 'dp')), parts along dimension 2
- grad_features: bfloat16 [64, 64, 512], P('pix', None, ('groups', 'dp')), parts along dimension 2
- grad_weights: float32 [8, 64, 64], P('groups'), parts along dimension 0
- grad_bias: float32 [128], P('groups'), parts along dimension 0
There are 2 independent parts, one for each index of `groups`. A program takes and returns all parts, laid end to end along the dimension named above; an argument that names none is the same for every part. Nothing has to cross between parts.
Inputs may be any that keep to these rules, and one draw needn't show every extreme that they name: `send_blocks`: for device p and direction d (to devices p + 1, p - 1, p + 2, p - 2 modulo 8, in this order), 2 distinct local block numbers of device p; no block is listed in two directions. `neighbours`: column 0 names a local block or a received slot 8 + d * 2 + s; every received slot is named by exactly one row, every local block by column 0 of at most one row. Column 1 names a local block other than the row's own, every local block by exactly one row. Both neighbour relations are symmetric. `lap_tiles`: the operator is symmetric: the tile of block b in the row of block a is the transpose of the tile of block a in the row of block b, and a block's own tile is symmetric.
All inputs are finite; a program needn't handle non-finite values. No bound on the sum of `pixel_mask` on one device may be relied on, other than what follows from the above.
Results may differ from a plain program's by a relative error of at most 0.0047.
Values may be sent and summed in bfloat16 or wider, within the bound.
No kernel may reach another device: no remote copies, remote signals or barrier semaphores. Data moves between devices by JAX's collectives and lax.ppermute only.
A program may use at most 64 MiB of HBM per device.

v0:
```python
import math
import jax
import jax.numpy as jnp
from jax import lax
from jax.sharding import PartitionSpec as P

DIRECTIONS = (1, -1, 2, -2)
CYCLE_STEPS = (0, -1, 1, -2, 2, -3, 3)


def shifted(block, axis, distance):
    devices = range(lax.axis_size(axis))
    route = [((i - distance) % len(devices), i) for i in devices]
    return lax.ppermute(block, axis, route)


def collect_halo(masked_values, outgoing):
    pieces = []
    for heading_index, travel in enumerate(DIRECTIONS):
        pieces.append(shifted(masked_values[outgoing[heading_index]], "pix", travel))
    return jnp.concatenate(pieces, axis=0)


def tile_product(masked_values, extended, lap_tiles, neighbours, keep_mask):
    block_count, pixel_count, lane_count = masked_values.shape
    columns = [jnp.roll(masked_values, -offset, axis=0) for offset in CYCLE_STEPS]
    columns.append(extended[neighbours[:, 0]])
    columns.append(extended[neighbours[:, 1]])
    picked = jnp.stack(columns, axis=1).reshape(block_count, -1, lane_count)
    product = jnp.einsum("bpk,bkl->bpl", lap_tiles, picked, preferred_element_type=jnp.float32)
    return product * keep_mask


def forward_apply(values, lap_tiles, neighbours, outgoing, keep_mask):
    masked_values = values * keep_mask
    halo_blocks = collect_halo(masked_values, outgoing)
    extended = jnp.concatenate([masked_values, halo_blocks], axis=0)
    return tile_product(masked_values, extended, lap_tiles, neighbours, keep_mask)


def pushed_apply(values, lap_tiles, neighbours, outgoing, keep_mask):
    masked_values = values * keep_mask
    block_count, pixel_count, lane_count = values.shape
    cycle_count = len(CYCLE_STEPS)
    partial_terms = jnp.einsum(
        "bpk,bpl->bkl", lap_tiles, masked_values, preferred_element_type=jnp.float32
    )
    partial_terms = partial_terms.reshape(block_count, -1, pixel_count, lane_count)
    running = jnp.zeros((block_count, pixel_count, lane_count), jnp.float32)
    for column, offset in enumerate(CYCLE_STEPS):
        running = running + jnp.roll(partial_terms[:, column], offset, axis=0)
    slot_count = outgoing.shape[1]
    halo_count = len(DIRECTIONS) * slot_count
    irregular = jnp.concatenate(
        [partial_terms[:, cycle_count], partial_terms[:, cycle_count + 1]], axis=0
    )
    target_ids = jnp.concatenate([neighbours[:, 0], neighbours[:, 1]], axis=0)
    pooled = jax.ops.segment_sum(irregular, target_ids, num_segments=block_count + halo_count)
    running = running + pooled[:block_count]
    returned_all = pooled[block_count:].reshape(
        len(DIRECTIONS), slot_count, pixel_count, lane_count
    )
    for heading_index, travel in enumerate(DIRECTIONS):
        returned = shifted(returned_all[heading_index], "pix", -travel)
        running = running.at[outgoing[heading_index]].add(returned)
    return running * keep_mask


def local(
    features, cheb_weights, out_bias, lap_tiles, neighbours, send_blocks, pixel_mask, cotangent
):
    block_count, pixel_count, lane_count = features.shape
    term_count, chan_in, chan_out = cheb_weights.shape
    map_count = lane_count // chan_in
    outgoing = send_blocks[0]
    keep_mask = pixel_mask.astype(jnp.bfloat16)[:, :, None]
    cheb_terms = [features]
    for degree in range(1, term_count):
        applied = forward_apply(cheb_terms[-1], lap_tiles, neighbours, outgoing, keep_mask)
        if degree == 1:
            cheb_terms.append(applied.astype(jnp.bfloat16))
        else:
            cheb_terms.append((2.0 * applied - cheb_terms[-2]).astype(jnp.bfloat16))
    flat_rows = block_count * pixel_count
    mixed_sum = jnp.zeros((flat_rows, map_count, chan_out), jnp.float32)
    for degree in range(term_count):
        term_block = cheb_terms[degree].reshape(flat_rows, map_count, chan_in)
        mixed_sum = mixed_sum + jnp.einsum(
            "rmc,co->rmo", term_block, cheb_weights[degree], preferred_element_type=jnp.float32
        )
    output_maps = (
        (mixed_sum + out_bias)
        .reshape(block_count, pixel_count, map_count * chan_out)
        .astype(jnp.bfloat16)
    )
    upstream = cotangent.reshape(flat_rows, map_count, chan_out)

    def direct(degree):
        return jnp.einsum(
            "rmo,co->rmc", upstream, cheb_weights[degree], preferred_element_type=jnp.float32
        ).reshape(block_count, pixel_count, lane_count)

    def adjoint(values):
        return pushed_apply(values, lap_tiles, neighbours, outgoing, keep_mask)

    adjoints = [None] * term_count
    for degree in range(term_count - 1, 0, -1):
        running = direct(degree)
        if degree + 1 < term_count:
            running = running + 2.0 * adjoint(adjoints[degree + 1])
        if degree + 2 < term_count:
            running = running - adjoints[degree + 2]
        adjoints[degree] = running.astype(jnp.bfloat16)
    running = direct(0) + adjoint(adjoints[1]) - adjoints[2]
    grad_features = running.astype(jnp.bfloat16)
    grad_list = []
    for degree in range(term_count):
        term_block = cheb_terms[degree].reshape(flat_rows, map_count, chan_in)
        grad_list.append(
            jnp.einsum("rmc,rmo->co", term_block, upstream, preferred_element_type=jnp.float32)
        )
    partial_grads = jnp.stack(grad_list)
    bias_part = jnp.sum(upstream.astype(jnp.float32), axis=(0, 1))
    summed_weights, summed_bias = lax.psum((partial_grads, bias_part), ("pix", "dp"))
    factor = 1.0 / math.sqrt(flat_rows * map_count * lax.axis_size("pix") * lax.axis_size("dp"))
    return (output_maps, grad_features, summed_weights * factor, summed_bias * factor)


def solution(mesh):
    return jax.shard_map(
        local,
        mesh=mesh,
        in_specs=(
            P("pix", None, ("groups", "dp")),
            P(),
            P(),
            P("pix", None, None),
            P("pix", None),
            P("pix", None, None),
            P("pix", None),
            P("pix", None, ("groups", "dp")),
        ),
        out_specs=(
            P("pix", None, ("groups", "dp")),
            P("pix", None, ("groups", "dp")),
            P("groups", None, None),
            P("groups"),
        ),
        check_vma=False,
    )
```

profile of v0, /device:TPU:8, one launch (start us, length us, event | category | flops | bytes accessed | tf_op | source)
XLA Modules:
  0.0 317.3 jit_solution(6542873860701884093)
XLA Ops:
  26.8 3.0 scatter_fusion
  31.5 2.2 collective-permute-start.12
  52.8 24.3 %psum.15 = f32[64]{0:T(128)} all-reduce(f32[64]{0:T(128)} %reduce_sum.18), channel_id=1, replica_groups=mesh['groups'=2,'pix'=8,'dp'=2] {'pix','dp'}, use_global_device_ids=true, to_apply=%region_18.19 | all-reduce | flops 64 | bytes 512 | tf_op jit(solution)/shard_map/psum | solution.py:124
  93.6 7.7 %collective-permute-start.14 = (f32[2,64,128]{2,1,0:T(8,128)}, f32[2,64,128]{2,1,0:T(8,128)}, u32[]{:S(2)}, u32[]{:S(2)}) collective-permute-start(f32[2,64,128]{2,1,0:T(8,128)} %get-tuple-element.75), channel_id=1, source_target_pairs={{4,0},{6,2},{8,4},{10,6},{12,8},{14,10},{0,12},{2,14},{5,1},{7,3},... | collective-permute-start | bytes 196616 | tf_op jit(solution)/shard_map/ppermute | solution.py:14
  118.4 3.9 %collective-permute-start.5 = (bf16[2,64,128]{2,1,0:T(8,128)(2,1)S(1)}, bf16[2,64,128]{2,1,0:T(8,128)(2,1)S(1)}, u32[]{:S(2)}, u32[]{:S(2)}) collective-permute-start(bf16[2,64,128]{2,1,0:T(8,128)(2,1)S(1)} %gather_fusion.7), channel_id=1, source_target_pairs={{2,0},{4,2},{6,4},{8,6},{10,8},{12,10},{14,12},{0,14},{3,1},{5,3},... | collective-permute-start | bytes 98312 | tf_op jit(solution)/shard_map/ppermute | solution.py:14
  123.9 2.0 collective-permute-start.6
  125.9 3.7 %collective-permute-done.6 = bf16[2,64,128]{2,1,0:T(8,128)(2,1)S(1)} collective-permute-done((bf16[2,64,128]{2,1,0:T(8,128)(2,1)S(1)}, bf16[2,64,128]{2,1,0:T(8,128)(2,1)S(1)}, u32[]{:S(2)}, u32[]{:S(2)}) %collective-permute-start.6) | collective-permute-done | bytes 32800 | tf_op jit(solution)/shard_map/ppermute | solution.py:14
  129.6 3.9 %collective-permute-start.7 = (bf16[2,64,128]{2,1,0:T(8,128)(2,1)S(1)}, bf16[2,64,128]{2,1,0:T(8,128)(2,1)S(1)}, u32[]{:S(2)}, u32[]{:S(2)}) collective-permute-start(bf16[2,64,128]{2,1,0:T(8,128)(2,1)S(1)} %gather_fusion.9), channel_id=1, source_target_pairs={{4,0},{6,2},{8,4},{10,6},{12,8},{14,10},{0,12},{2,14},{5,1},{7,3},... | collective-permute-start | bytes 98312 | tf_op jit(solution)/shard_map/ppermute | solution.py:14
  160.2 2.0 collective-permute-start.8
  163.9 3.5 %collective-permute-start.11 = (bf16[2,64,128]{2,1,0:T(8,128)(2,1)}, bf16[2,64,128]{2,1,0:T(8,128)(2,1)}, u32[]{:S(2)}, u32[]{:S(2)}) collective-permute-start(bf16[2,64,128]{2,1,0:T(8,128)(2,1)} %gather_fusion.15), channel_id=1, source_target_pairs={{4,0},{6,2},{8,4},{10,6},{12,8},{14,10},{0,12},{2,14},{5,1},{7,3},... | collective-permute-start | bytes 98312 | tf_op jit(solution)/shard_map/ppermute | solution.py:14
  168.5 1.9 pad_maximum_fusion.1
  171.2 3.3 %scatter_fusion.5 = f32[16,64,128]{2,1,0:T(8,128)} fusion(f32[16,64,128]{2,1,0:T(8,128)} %broadcast.94.clone.1, s32[16]{0:T(128)} %copy-done.72, f32[16,64,128]{2,1,0:T(8,128)} %pad_maximum_fusion.1), kind=kCustom, calls=%fused_computation.23 | custom fusion | flops 131072 | bytes 1572928 | tf_op jit(solution)/shard_map/scatter-add | solution.py:58
  176.4 2.3 collective-permute-start.16
  190.2 3.5 %collective-permute-start.18 = (f32[2,64,128]{2,1,0:T(8,128)}, f32[2,64,128]{2,1,0:T(8,128)S(1)}, u32[]{:S(2)}, u32[]{:S(2)}) collective-permute-start(f32[2,64,128]{2,1,0:T(8,128)} %get-tuple-element.71), channel_id=1, source_target_pairs={{4,0},{6,2},{8,4},{10,6},{12,8},{14,10},{0,12},{2,14},{5,1},{7,3},... | collective-permute-start | bytes 196616 | tf_op jit(solution)/shard_map/ppermute | solution.py:14
  217.9 2.2 scatter_fusion.10
  220.8 3.0 collective-permute-start.20
  223.7 3.8 %collective-permute-start.22 = (f32[2,64,128]{2,1,0:T(8,128)}, f32[2,64,128]{2,1,0:T(8,128)}, u32[]{:S(2)}, u32[]{:S(2)}) collective-permute-start(f32[2,64,128]{2,1,0:T(8,128)} %get-tuple-element.67), channel_id=1, source_target_pairs={{4,0},{6,2},{8,4},{10,6},{12,8},{14,10},{0,12},{2,14},{5,1},{7,3},... | collective-permute-start | bytes 196616 | tf_op jit(solution)/shard_map/ppermute | solution.py:14
  227.6 2.3 slice_add_fusion
  229.9 68.8 %all-reduce.2.cloned.1.call-done = f32[4,64,64]{2,1,0:T(8,128)} async-done(((f32[4,64,64]{2,1,0:T(8,128)}), f32[4,64,64]{2,1,0:T(8,128)}) %all-reduce.2.cloned.1.call-update) | async-done | bytes 65552 | tf_op jit(solution)/shard_map/psum | solution.py:124
  300.2 2.1 scatter_fusion.11
  302.3 2.1 scatter_fusion.12
  304.4 2.2 scatter_fusion.13
  306.6 2.1 scatter_fusion.14
  308.7 1.8 subtract_convert_fusion
  (366 shorter events, 144.5 us)
Async XLA Ops:
  7.2 291.5 %all-reduce.2.cloned.1.call-start = ((), (), s32[]{:S(2)}) async-start(), calls=%async_computation | async-start | bytes 262144 | tf_op jit(solution)/shard_map/psum | solution.py:124
  11.9 80.9 %collective-permute-start = (bf16[2,64,128]{2,1,0:T(8,128)(2,1)}, bf16[2,64,128]{2,1,0:T(8,128)(2,1)}, u32[]{:S(2)}, u32[]{:S(2)}) collective-permute-start(bf16[2,64,128]{2,1,0:T(8,128)(2,1)} %gather_fusion), channel_id=1, source_target_pairs={{14,0},{0,2},{2,4},{4,6},{6,8},{8,10},{10,12},{12,14},{15,1},{1,3}... | collective-permute-start | bytes 98312 | tf_op jit(solution)/shard_map/ppermute | solution.py:14
  14.6 79.0 %collective-permute-start.1 = (bf16[2,64,128]{2,1,0:T(8,128)(2,1)}, bf16[2,64,128]{2,1,0:T(8,128)(2,1)}, u32[]{:S(2)}, u32[]{:S(2)}) collective-permute-start(bf16[2,64,128]{2,1,0:T(8,128)(2,1)} %gather_fusion.1), channel_id=1, source_target_pairs={{2,0},{4,2},{6,4},{8,6},{10,8},{12,10},{14,12},{0,14},{3,1},{5,3},... | collective-permute-start | bytes 98312 | tf_op jit(solution)/shard_map/ppermute | solution.py:14
  17.3 84.8 %collective-permute-start.2 = (bf16[2,64,128]{2,1,0:T(8,128)(2,1)}, bf16[2,64,128]{2,1,0:T(8,128)(2,1)}, u32[]{:S(2)}, u32[]{:S(2)}) collective-permute-start(bf16[2,64,128]{2,1,0:T(8,128)(2,1)} %gather_fusion.2), channel_id=1, source_target_pairs={{12,0},{14,2},{0,4},{2,6},{4,8},{6,10},{8,12},{10,14},{13,1},{15,3... | collective-permute-start | bytes 98312 | tf_op jit(solution)/shard_map/ppermute | solution.py:14
  20.0 82.9 %collective-permute-start.3 = (bf16[2,64,128]{2,1,0:T(8,128)(2,1)}, bf16[2,64,128]{2,1,0:T(8,128)(2,1)}, u32[]{:S(2)}, u32[]{:S(2)}) collective-permute-start(bf16[2,64,128]{2,1,0:T(8,128)(2,1)} %gather_fusion.3), channel_id=1, source_target_pairs={{4,0},{6,2},{8,4},{10,6},{12,8},{14,10},{0,12},{2,14},{5,1},{7,3},... | collective-permute-start | bytes 98312 | tf_op jit(solution)/shard_map/ppermute | solution.py:14
  31.5 116.9 %collective-permute-start.12 = (f32[2,64,128]{2,1,0:T(8,128)}, f32[2,64,128]{2,1,0:T(8,128)}, u32[]{:S(2)}, u32[]{:S(2)}) collective-permute-start(f32[2,64,128]{2,1,0:T(8,128)} %get-tuple-element.77), channel_id=1, source_target_pairs={{2,0},{4,2},{6,4},{8,6},{10,8},{12,10},{14,12},{0,14},{3,1},{5,3},... | collective-permute-start | bytes 196616 | tf_op jit(solution)/shard_map/ppermute | solution.py:14
  92.9 57.0 %collective-permute-start.13 = (f32[2,64,128]{2,1,0:T(8,128)}, f32[2,64,128]{2,1,0:T(8,128)}, u32[]{:S(2)}, u32[]{:S(2)}) collective-permute-start(f32[2,64,128]{2,1,0:T(8,128)} %get-tuple-element.76), channel_id=1, source_target_pairs={{14,0},{0,2},{2,4},{4,6},{6,8},{8,10},{10,12},{12,14},{15,1},{1,3}... | collective-permute-start | bytes 196616 | tf_op jit(solution)/shard_map/ppermute | solution.py:14
  93.6 57.7 %collective-permute-start.14 = (f32[2,64,128]{2,1,0:T(8,128)}, f32[2,64,128]{2,1,0:T(8,128)}, u32[]{:S(2)}, u32[]{:S(2)}) collective-permute-start(f32[2,64,128]{2,1,0:T(8,128)} %get-tuple-element.75), channel_id=1, source_target_pairs={{4,0},{6,2},{8,4},{10,6},{12,8},{14,10},{0,12},{2,14},{5,1},{7,3},... | collective-permute-start | bytes 196616 | tf_op jit(solution)/shard_map/ppermute | solution.py:14
  102.1 50.7 %collective-permute-start.15 = (f32[2,64,128]{2,1,0:T(8,128)}, f32[2,64,128]{2,1,0:T(8,128)}, u32[]{:S(2)}, u32[]{:S(2)}) collective-permute-start(f32[2,64,128]{2,1,0:T(8,128)} %get-tuple-element.74), channel_id=1, source_target_pairs={{12,0},{14,2},{0,4},{2,6},{4,8},{6,10},{8,12},{10,14},{13,1},{15,3... | collective-permute-start | bytes 196616 | tf_op jit(solution)/shard_map/ppermute | solution.py:14
  111.5 6.9 %collective-permute-start.4 = (bf16[2,64,128]{2,1,0:T(8,128)(2,1)}, bf16[2,64,128]{2,1,0:T(8,128)(2,1)}, u32[]{:S(2)}, u32[]{:S(2)}) collective-permute-start(bf16[2,64,128]{2,1,0:T(8,128)(2,1)} %gather_fusion.6), channel_id=1, source_target_pairs={{14,0},{0,2},{2,4},{4,6},{6,8},{8,10},{10,12},{12,14},{15,1},{1,3}... | collective-permute-start | bytes 98312 | tf_op jit(solution)/shard_map/ppermute | solution.py:14
  123.9 5.7 %collective-permute-start.6 = (bf16[2,64,128]{2,1,0:T(8,128)(2,1)S(1)}, bf16[2,64,128]{2,1,0:T(8,128)(2,1)S(1)}, u32[]{:S(2)}, u32[]{:S(2)}) collective-permute-start(bf16[2,64,128]{2,1,0:T(8,128)(2,1)S(1)} %gather_fusion.8), channel_id=1, source_target_pairs={{12,0},{14,2},{0,4},{2,6},{4,8},{6,10},{8,12},{10,14},{13,1},{15,3... | collective-permute-start | bytes 98312 | tf_op jit(solution)/shard_map/ppermute | solution.py:14
  129.6 5.5 %collective-permute-start.7 = (bf16[2,64,128]{2,1,0:T(8,128)(2,1)S(1)}, bf16[2,64,128]{2,1,0:T(8,128)(2,1)S(1)}, u32[]{:S(2)}, u32[]{:S(2)}) collective-permute-start(bf16[2,64,128]{2,1,0:T(8,128)(2,1)S(1)} %gather_fusion.9), channel_id=1, source_target_pairs={{4,0},{6,2},{8,4},{10,6},{12,8},{14,10},{0,12},{2,14},{5,1},{7,3},... | collective-permute-start | bytes 98312 | tf_op jit(solution)/shard_map/ppermute | solution.py:14
  160.2 28.7 %collective-permute-start.8 = (bf16[2,64,128]{2,1,0:T(8,128)(2,1)}, bf16[2,64,128]{2,1,0:T(8,128)(2,1)}, u32[]{:S(2)}, u32[]{:S(2)}) collective-permute-start(bf16[2,64,128]{2,1,0:T(8,128)(2,1)} %gather_fusion.12), channel_id=1, source_target_pairs={{14,0},{0,2},{2,4},{4,6},{6,8},{8,10},{10,12},{12,14},{15,1},{1,3}... | collective-permute-start | bytes 98312 | tf_op jit(solution)/shard_map/ppermute | solution.py:14
  162.1 28.1 %collective-permute-start.9 = (bf16[2,64,128]{2,1,0:T(8,128)(2,1)}, bf16[2,64,128]{2,1,0:T(8,128)(2,1)}, u32[]{:S(2)}, u32[]{:S(2)}) collective-permute-start(bf16[2,64,128]{2,1,0:T(8,128)(2,1)} %gather_fusion.13), channel_id=1, source_target_pairs={{2,0},{4,2},{6,4},{8,6},{10,8},{12,10},{14,12},{0,14},{3,1},{5,3},... | collective-permute-start | bytes 98312 | tf_op jit(solution)/shard_map/ppermute | solution.py:14
  163.9 31.2 %collective-permute-start.10 = (bf16[2,64,128]{2,1,0:T(8,128)(2,1)}, bf16[2,64,128]{2,1,0:T(8,128)(2,1)}, u32[]{:S(2)}, u32[]{:S(2)}) collective-permute-start(bf16[2,64,128]{2,1,0:T(8,128)(2,1)} %gather_fusion.14), channel_id=1, source_target_pairs={{12,0},{14,2},{0,4},{2,6},{4,8},{6,10},{8,12},{10,14},{13,1},{15,3... | collective-permute-start | bytes 98312 | tf_op jit(solution)/shard_map/ppermute | solution.py:14
  163.9 32.6 %collective-permute-start.11 = (bf16[2,64,128]{2,1,0:T(8,128)(2,1)}, bf16[2,64,128]{2,1,0:T(8,128)(2,1)}, u32[]{:S(2)}, u32[]{:S(2)}) collective-permute-start(bf16[2,64,128]{2,1,0:T(8,128)(2,1)} %gather_fusion.15), channel_id=1, source_target_pairs={{4,0},{6,2},{8,4},{10,6},{12,8},{14,10},{0,12},{2,14},{5,1},{7,3},... | collective-permute-start | bytes 98312 | tf_op jit(solution)/shard_map/ppermute | solution.py:14
  176.4 31.1 %collective-permute-start.16 = (f32[2,64,128]{2,1,0:T(8,128)}, f32[2,64,128]{2,1,0:T(8,128)}, u32[]{:S(2)}, u32[]{:S(2)}) collective-permute-start(f32[2,64,128]{2,1,0:T(8,128)} %get-tuple-element.73), channel_id=1, source_target_pairs={{2,0},{4,2},{6,4},{8,6},{10,8},{12,10},{14,12},{0,14},{3,1},{5,3},... | collective-permute-start | bytes 196616 | tf_op jit(solution)/shard_map/ppermute | solution.py:14
  188.9 20.1 %collective-permute-start.17 = (f32[2,64,128]{2,1,0:T(8,128)}, f32[2,64,128]{2,1,0:T(8,128)S(1)}, u32[]{:S(2)}, u32[]{:S(2)}) collective-permute-start(f32[2,64,128]{2,1,0:T(8,128)} %get-tuple-element.72), channel_id=1, source_target_pairs={{14,0},{0,2},{2,4},{4,6},{6,8},{8,10},{10,12},{12,14},{15,1},{1,3}... | collective-permute-start | bytes 196616 | tf_op jit(solution)/shard_map/ppermute | solution.py:14
  190.2 19.4 %collective-permute-start.18 = (f32[2,64,128]{2,1,0:T(8,128)}, f32[2,64,128]{2,1,0:T(8,128)S(1)}, u32[]{:S(2)}, u32[]{:S(2)}) collective-permute-start(f32[2,64,128]{2,1,0:T(8,128)} %get-tuple-element.71), channel_id=1, source_target_pairs={{4,0},{6,2},{8,4},{10,6},{12,8},{14,10},{0,12},{2,14},{5,1},{7,3},... | collective-permute-start | bytes 196616 | tf_op jit(solution)/shard_map/ppermute | solution.py:14
  195.1 15.2 %collective-permute-start.19 = (f32[2,64,128]{2,1,0:T(8,128)}, f32[2,64,128]{2,1,0:T(8,128)S(1)}, u32[]{:S(2)}, u32[]{:S(2)}) collective-permute-start(f32[2,64,128]{2,1,0:T(8,128)} %get-tuple-element.70), channel_id=1, source_target_pairs={{12,0},{14,2},{0,4},{2,6},{4,8},{6,10},{8,12},{10,14},{13,1},{15,3... | collective-permute-start | bytes 196616 | tf_op jit(solution)/shard_map/ppermute | solution.py:14
  220.8 79.5 %collective-permute-start.20 = (f32[2,64,128]{2,1,0:T(8,128)}, f32[2,64,128]{2,1,0:T(8,128)}, u32[]{:S(2)}, u32[]{:S(2)}) collective-permute-start(f32[2,64,128]{2,1,0:T(8,128)} %get-tuple-element.69), channel_id=1, source_target_pairs={{2,0},{4,2},{6,4},{8,6},{10,8},{12,10},{14,12},{0,14},{3,1},{5,3},... | collective-permute-start | bytes 196616 | tf_op jit(solution)/shard_map/ppermute | solution.py:14
  223.7 78.6 %collective-permute-start.21 = (f32[2,64,128]{2,1,0:T(8,128)}, f32[2,64,128]{2,1,0:T(8,128)}, u32[]{:S(2)}, u32[]{:S(2)}) collective-permute-start(f32[2,64,128]{2,1,0:T(8,128)} %get-tuple-element.68), channel_id=1, source_target_pairs={{14,0},{0,2},{2,4},{4,6},{6,8},{8,10},{10,12},{12,14},{15,1},{1,3}... | collective-permute-start | bytes 196616 | tf_op jit(solution)/shard_map/ppermute | solution.py:14
  223.7 80.6 %collective-permute-start.22 = (f32[2,64,128]{2,1,0:T(8,128)}, f32[2,64,128]{2,1,0:T(8,128)}, u32[]{:S(2)}, u32[]{:S(2)}) collective-permute-start(f32[2,64,128]{2,1,0:T(8,128)} %get-tuple-element.67), channel_id=1, source_target_pairs={{4,0},{6,2},{8,4},{10,6},{12,8},{14,10},{0,12},{2,14},{5,1},{7,3},... | collective-permute-start | bytes 196616 | tf_op jit(solution)/shard_map/ppermute | solution.py:14
  227.6 79.0 %collective-permute-start.23 = (f32[2,64,128]{2,1,0:T(8,128)}, f32[2,64,128]{2,1,0:T(8,128)}, u32[]{:S(2)}, u32[]{:S(2)}) collective-permute-start(f32[2,64,128]{2,1,0:T(8,128)} %get-tuple-element.66), channel_id=1, source_target_pairs={{12,0},{14,2},{0,4},{2,6},{4,8},{6,10},{8,12},{10,14},{13,1},{15,3... | collective-permute-start | bytes 196616 | tf_op jit(solution)/shard_map/ppermute | solution.py:14
  (78 other events, 833.6 us)
Sparse Core Ops, SparseCore 0:
  205.7 92.9 all-reduce.1
where the time goes:
time: 320 us; the launch traced here: 317 us
  local copies, waits for them, and re-layouts  76.6 us (24%)
  waiting for transfers between devices  75.9 us (24%)
  other arithmetic  63.2 us (20%)
  starting transfers between devices  44.7 us (14%)
  blocking collectives  24.3 us (8%)
  matrix products  17.3 us (5%)
  between operations  15.4 us (5%)
    psum x1, waiting for transfers between devices, local(): lax.psum((partial_grads, bias_part), ('pix', 'dp'))  68.8 us
    ppermute x24, starting transfers between devices, shifted(): return lax.ppermute(block, axis, route)  44.6 us
    psum x1, blocking collectives, local(): lax.psum((partial_grads, bias_part), ('pix', 'dp'))  24.3 us
    unnamed x19, other arithmetic  19.2 us
    scatter-add x12, other arithmetic, pushed_apply(): running = running.at[outgoing[heading_index]].add(returned)  17.4 us
    gather x12, local copies, waits for them, and re-layouts, collect_halo(): masked_values[outgoing[heading_index]]  13.1 us
    slice x18, local copies, waits for them, and re-layouts, pushed_apply(): running = running + jnp.roll(partial_terms[:, column], offset, axis=0)  13 us
    unnamed x170, local copies, waits for them, and re-layouts  12 us
  transfers between devices with their start and end apart: 25, of which 5 were waited for; matrix products, arithmetic and copies ran while one was open for 44% of the time, Pallas kernels for 0%

commit v1 on v0

--- a/solution.py
+++ b/solution.py
@@ -121,7 +121,12 @@
         )
     partial_grads = jnp.stack(grad_list)
     bias_part = jnp.sum(upstream.astype(jnp.float32), axis=(0, 1))
-    summed_weights, summed_bias = lax.psum((partial_grads, bias_part), ("pix", "dp"))
+
+    def step_on_the_bench(page, mesh_ax, axis_tag):
+        local_out = lax.psum(page, axis_name=mesh_ax)
+        return lax.psum(local_out, axis_name=axis_tag)
+
+    summed_weights, summed_bias = step_on_the_bench((partial_grads, bias_part), "dp", "pix")
     factor = 1.0 / math.sqrt(flat_rows * map_count * lax.axis_size("pix") * lax.axis_size("dp"))
     return (output_maps, grad_features, summed_weights * factor, summed_bias * factor)
 

time: 320 us -> 310 us (0.969)
  waiting for transfers between devices: 75.9 us -> 70.8 us
  starting transfers between devices: 44.7 us -> 40.5 us
    psum x1 -> x2, waiting for transfers between devices: 68.8 us -> 63.9 us  [the longest x1 63.9 us: step_on_the_bench(): return lax.psum(local_out, axis_name=axis_tag)]
    ppermute x24, starting transfers between devices: 44.6 us -> 40.4 us  [shifted(): return lax.ppermute(block, axis, route)]
    psum x1 -> x2, blocking collectives: 24.3 us -> 21.2 us  [the longest x1 18.1 us: step_on_the_bench(): return lax.psum(local_out, axis_name=axis_tag)]
    unnamed x170 -> x168, local copies, waits for them, and re-layouts: 12 us -> 12 us
  transfers between devices with their start and end apart: 25 -> 26, of which waited for: 5 -> 5; matrix products, arithmetic and copies ran while one was open for 44% -> 46% of each run, Pallas kernels for 0% -> 0%
where the time goes in v1:
time: 310 us; the launch traced here: 305 us
  local copies, waits for them, and re-layouts  76.7 us (25%)
  waiting for transfers between devices  70.8 us (23%)
  other arithmetic  63.3 us (20%)
  starting transfers between devices  40.5 us (13%)
  blocking collectives  21.2 us (7%)
  matrix products  17.3 us (6%)
  between operations  15.4 us (5%)
    psum x1, waiting for transfers between devices, step_on_the_bench(): return lax.psum(local_out, axis_name=axis_tag)  63.9 us
    ppermute x24, starting transfers between devices, shifted(): return lax.ppermute(block, axis, route)  40.4 us
    unnamed x19, other arithmetic  19.2 us
    psum x1, blocking collectives, step_on_the_bench(): return lax.psum(local_out, axis_name=axis_tag)  18.1 us
    scatter-add x12, other arithmetic, pushed_apply(): running = running.at[outgoing[heading_index]].add(returned)  17.4 us
    slice x18, local copies, waits for them, and re-layouts, pushed_apply(): running = running + jnp.roll(partial_terms[:, column], offset, axis=0)  13.1 us
    gather x12, local copies, waits for them, and re-layouts, collect_halo(): masked_values[outgoing[heading_index]]  13 us
    unnamed x168, local copies, waits for them, and re-layouts  12 us
  transfers between devices with their start and end apart: 26, of which 5 were waited for; matrix products, arithmetic and copies ran while one was open for 46% of the time, Pallas kernels for 0%

profile of v1, /device:TPU:8, one launch (start us, length us, event | category | flops | bytes accessed | tf_op | source)
XLA Modules:
  0.0 305.1 jit_solution(8863353574309804598)
XLA Ops:
  26.8 3.0 scatter_fusion
  31.6 2.2 collective-permute-start.12
  53.0 3.1 %psum.30 = f32[64]{0:T(128)} all-reduce(f32[64]{0:T(128)} %reduce_sum.18), channel_id=1, replica_groups=mesh['groups'=2,'pix'=8,'dp'=2] {'dp'}, use_global_device_ids=true, to_apply=%region_19.20 | all-reduce | flops 64 | bytes 512 | tf_op jit(solution)/shard_map/psum | solution.py:126
  56.0 18.1 %psum.31 = f32[64]{0:T(128)} all-reduce(f32[64]{0:T(128)} %psum.30), channel_id=1, replica_groups=mesh['groups'=2,'pix'=8,'dp'=2] {'pix'}, use_global_device_ids=true, to_apply=%region_20.21 | all-reduce | flops 64 | bytes 512 | tf_op jit(solution)/shard_map/psum | solution.py:127
  90.8 3.3 %collective-permute-start.14 = (f32[2,64,128]{2,1,0:T(8,128)}, f32[2,64,128]{2,1,0:T(8,128)}, u32[]{:S(2)}, u32[]{:S(2)}) collective-permute-start(f32[2,64,128]{2,1,0:T(8,128)} %get-tuple-element.75), channel_id=1, source_target_pairs={{4,0},{6,2},{8,4},{10,6},{12,8},{14,10},{0,12},{2,14},{5,1},{7,3},... | collective-permute-start | bytes 196616 | tf_op jit(solution)/shard_map/ppermute | solution.py:14
  111.0 3.9 %collective-permute-start.5 = (bf16[2,64,128]{2,1,0:T(8,128)(2,1)S(1)}, bf16[2,64,128]{2,1,0:T(8,128)(2,1)S(1)}, u32[]{:S(2)}, u32[]{:S(2)}) collective-permute-start(bf16[2,64,128]{2,1,0:T(8,128)(2,1)S(1)} %gather_fusion.7), channel_id=1, source_target_pairs={{2,0},{4,2},{6,4},{8,6},{10,8},{12,10},{14,12},{0,14},{3,1},{5,3},... | collective-permute-start | bytes 98312 | tf_op jit(solution)/shard_map/ppermute | solution.py:14
  116.5 2.0 collective-permute-start.6
  118.5 3.7 %collective-permute-done.6 = bf16[2,64,128]{2,1,0:T(8,128)(2,1)S(1)} collective-permute-done((bf16[2,64,128]{2,1,0:T(8,128)(2,1)S(1)}, bf16[2,64,128]{2,1,0:T(8,128)(2,1)S(1)}, u32[]{:S(2)}, u32[]{:S(2)}) %collective-permute-start.6) | collective-permute-done | bytes 32800 | tf_op jit(solution)/shard_map/ppermute | solution.py:14
  122.2 3.8 %collective-permute-start.7 = (bf16[2,64,128]{2,1,0:T(8,128)(2,1)S(1)}, bf16[2,64,128]{2,1,0:T(8,128)(2,1)S(1)}, u32[]{:S(2)}, u32[]{:S(2)}) collective-permute-start(bf16[2,64,128]{2,1,0:T(8,128)(2,1)S(1)} %gather_fusion.9), channel_id=1, source_target_pairs={{4,0},{6,2},{8,4},{10,6},{12,8},{14,10},{0,12},{2,14},{5,1},{7,3},... | collective-permute-start | bytes 98312 | tf_op jit(solution)/shard_map/ppermute | solution.py:14
  156.2 3.8 %collective-permute-start.11 = (bf16[2,64,128]{2,1,0:T(8,128)(2,1)}, bf16[2,64,128]{2,1,0:T(8,128)(2,1)}, u32[]{:S(2)}, u32[]{:S(2)}) collective-permute-start(bf16[2,64,128]{2,1,0:T(8,128)(2,1)} %gather_fusion.15), channel_id=1, source_target_pairs={{4,0},{6,2},{8,4},{10,6},{12,8},{14,10},{0,12},{2,14},{5,1},{7,3},... | collective-permute-start | bytes 98312 | tf_op jit(solution)/shard_map/ppermute | solution.py:14
  161.1 1.9 pad_maximum_fusion.1
  163.8 3.3 %scatter_fusion.5 = f32[16,64,128]{2,1,0:T(8,128)} fusion(f32[16,64,128]{2,1,0:T(8,128)} %broadcast.94.clone.1, s32[16]{0:T(128)} %copy-done.71, f32[16,64,128]{2,1,0:T(8,128)} %pad_maximum_fusion.1), kind=kCustom, calls=%fused_computation.23 | custom fusion | flops 131072 | bytes 1572928 | tf_op jit(solution)/shard_map/scatter-add | solution.py:58
  169.0 2.0 collective-permute-start.16
  182.5 3.8 %collective-permute-start.18 = (f32[2,64,128]{2,1,0:T(8,128)}, f32[2,64,128]{2,1,0:T(8,128)S(1)}, u32[]{:S(2)}, u32[]{:S(2)}) collective-permute-start(f32[2,64,128]{2,1,0:T(8,128)} %get-tuple-element.71), channel_id=1, source_target_pairs={{4,0},{6,2},{8,4},{10,6},{12,8},{14,10},{0,12},{2,14},{5,1},{7,3},... | collective-permute-start | bytes 196616 | tf_op jit(solution)/shard_map/ppermute | solution.py:14
  210.5 2.2 scatter_fusion.10
  213.4 2.9 collective-permute-start.20
  216.3 3.8 %collective-permute-start.22 = (f32[2,64,128]{2,1,0:T(8,128)}, f32[2,64,128]{2,1,0:T(8,128)}, u32[]{:S(2)}, u32[]{:S(2)}) collective-permute-start(f32[2,64,128]{2,1,0:T(8,128)} %get-tuple-element.67), channel_id=1, source_target_pairs={{4,0},{6,2},{8,4},{10,6},{12,8},{14,10},{0,12},{2,14},{5,1},{7,3},... | collective-permute-start | bytes 196616 | tf_op jit(solution)/shard_map/ppermute | solution.py:14
  220.1 2.3 slice_add_fusion
  222.5 2.1 scatter_fusion.11
  224.5 2.1 scatter_fusion.12
  226.6 2.2 scatter_fusion.13
  228.8 2.1 scatter_fusion.14
  230.9 1.9 subtract_convert_fusion
  232.8 63.9 %all-reduce.5.cloned.1.call-done = f32[4,64,64]{2,1,0:T(8,128)} async-done(((f32[4,64,64]{2,1,0:T(8,128)}), f32[4,64,64]{2,1,0:T(8,128)}) %all-reduce.5.cloned.1.call-update) | async-done | bytes 65552 | tf_op jit(solution)/shard_map/psum | solution.py:127
  (368 shorter events, 146.4 us)
Async XLA Ops:
  7.2 215.2 %all-reduce.3.cloned.1.call-start = ((), (), s32[]{:S(2)}) async-start(), calls=%async_computation | async-start | bytes 262144 | tf_op jit(solution)/shard_map/psum | solution.py:126
  11.9 77.9 %collective-permute-start = (bf16[2,64,128]{2,1,0:T(8,128)(2,1)}, bf16[2,64,128]{2,1,0:T(8,128)(2,1)}, u32[]{:S(2)}, u32[]{:S(2)}) collective-permute-start(bf16[2,64,128]{2,1,0:T(8,128)(2,1)} %gather_fusion), channel_id=1, source_target_pairs={{14,0},{0,2},{2,4},{4,6},{6,8},{8,10},{10,12},{12,14},{15,1},{1,3}... | collective-permute-start | bytes 98312 | tf_op jit(solution)/shard_map/ppermute | solution.py:14
  14.6 76.2 %collective-permute-start.1 = (bf16[2,64,128]{2,1,0:T(8,128)(2,1)}, bf16[2,64,128]{2,1,0:T(8,128)(2,1)}, u32[]{:S(2)}, u32[]{:S(2)}) collective-permute-start(bf16[2,64,128]{2,1,0:T(8,128)(2,1)} %gather_fusion.1), channel_id=1, source_target_pairs={{2,0},{4,2},{6,4},{8,6},{10,8},{12,10},{14,12},{0,14},{3,1},{5,3},... | collective-permute-start | bytes 98312 | tf_op jit(solution)/shard_map/ppermute | solution.py:14
  17.2 77.7 %collective-permute-start.2 = (bf16[2,64,128]{2,1,0:T(8,128)(2,1)}, bf16[2,64,128]{2,1,0:T(8,128)(2,1)}, u32[]{:S(2)}, u32[]{:S(2)}) collective-permute-start(bf16[2,64,128]{2,1,0:T(8,128)(2,1)} %gather_fusion.2), channel_id=1, source_target_pairs={{12,0},{14,2},{0,4},{2,6},{4,8},{6,10},{8,12},{10,14},{13,1},{15,3... | collective-permute-start | bytes 98312 | tf_op jit(solution)/shard_map/ppermute | solution.py:14
  20.0 75.8 %collective-permute-start.3 = (bf16[2,64,128]{2,1,0:T(8,128)(2,1)}, bf16[2,64,128]{2,1,0:T(8,128)(2,1)}, u32[]{:S(2)}, u32[]{:S(2)}) collective-permute-start(bf16[2,64,128]{2,1,0:T(8,128)(2,1)} %gather_fusion.3), channel_id=1, source_target_pairs={{4,0},{6,2},{8,4},{10,6},{12,8},{14,10},{0,12},{2,14},{5,1},{7,3},... | collective-permute-start | bytes 98312 | tf_op jit(solution)/shard_map/ppermute | solution.py:14
  31.6 109.3 %collective-permute-start.12 = (f32[2,64,128]{2,1,0:T(8,128)}, f32[2,64,128]{2,1,0:T(8,128)}, u32[]{:S(2)}, u32[]{:S(2)}) collective-permute-start(f32[2,64,128]{2,1,0:T(8,128)} %get-tuple-element.77), channel_id=1, source_target_pairs={{2,0},{4,2},{6,4},{8,6},{10,8},{12,10},{14,12},{0,14},{3,1},{5,3},... | collective-permute-start | bytes 196616 | tf_op jit(solution)/shard_map/ppermute | solution.py:14
  89.8 52.5 %collective-permute-start.13 = (f32[2,64,128]{2,1,0:T(8,128)}, f32[2,64,128]{2,1,0:T(8,128)}, u32[]{:S(2)}, u32[]{:S(2)}) collective-permute-start(f32[2,64,128]{2,1,0:T(8,128)} %get-tuple-element.76), channel_id=1, source_target_pairs={{14,0},{0,2},{2,4},{4,6},{6,8},{8,10},{10,12},{12,14},{15,1},{1,3}... | collective-permute-start | bytes 196616 | tf_op jit(solution)/shard_map/ppermute | solution.py:14
  90.8 52.9 %collective-permute-start.14 = (f32[2,64,128]{2,1,0:T(8,128)}, f32[2,64,128]{2,1,0:T(8,128)}, u32[]{:S(2)}, u32[]{:S(2)}) collective-permute-start(f32[2,64,128]{2,1,0:T(8,128)} %get-tuple-element.75), channel_id=1, source_target_pairs={{4,0},{6,2},{8,4},{10,6},{12,8},{14,10},{0,12},{2,14},{5,1},{7,3},... | collective-permute-start | bytes 196616 | tf_op jit(solution)/shard_map/ppermute | solution.py:14
  94.9 50.3 %collective-permute-start.15 = (f32[2,64,128]{2,1,0:T(8,128)}, f32[2,64,128]{2,1,0:T(8,128)}, u32[]{:S(2)}, u32[]{:S(2)}) collective-permute-start(f32[2,64,128]{2,1,0:T(8,128)} %get-tuple-element.74), channel_id=1, source_target_pairs={{12,0},{14,2},{0,4},{2,6},{4,8},{6,10},{8,12},{10,14},{13,1},{15,3... | collective-permute-start | bytes 196616 | tf_op jit(solution)/shard_map/ppermute | solution.py:14
  104.3 6.7 %collective-permute-start.4 = (bf16[2,64,128]{2,1,0:T(8,128)(2,1)}, bf16[2,64,128]{2,1,0:T(8,128)(2,1)}, u32[]{:S(2)}, u32[]{:S(2)}) collective-permute-start(bf16[2,64,128]{2,1,0:T(8,128)(2,1)} %gather_fusion.6), channel_id=1, source_target_pairs={{14,0},{0,2},{2,4},{4,6},{6,8},{8,10},{10,12},{12,14},{15,1},{1,3}... | collective-permute-start | bytes 98312 | tf_op jit(solution)/shard_map/ppermute | solution.py:14
  116.5 5.7 %collective-permute-start.6 = (bf16[2,64,128]{2,1,0:T(8,128)(2,1)S(1)}, bf16[2,64,128]{2,1,0:T(8,128)(2,1)S(1)}, u32[]{:S(2)}, u32[]{:S(2)}) collective-permute-start(bf16[2,64,128]{2,1,0:T(8,128)(2,1)S(1)} %gather_fusion.8), channel_id=1, source_target_pairs={{12,0},{14,2},{0,4},{2,6},{4,8},{6,10},{8,12},{10,14},{13,1},{15,3... | collective-permute-start | bytes 98312 | tf_op jit(solution)/shard_map/ppermute | solution.py:14
  152.7 28.5 %collective-permute-start.8 = (bf16[2,64,128]{2,1,0:T(8,128)(2,1)}, bf16[2,64,128]{2,1,0:T(8,128)(2,1)}, u32[]{:S(2)}, u32[]{:S(2)}) collective-permute-start(bf16[2,64,128]{2,1,0:T(8,128)(2,1)} %gather_fusion.12), channel_id=1, source_target_pairs={{14,0},{0,2},{2,4},{4,6},{6,8},{8,10},{10,12},{12,14},{15,1},{1,3}... | collective-permute-start | bytes 98312 | tf_op jit(solution)/shard_map/ppermute | solution.py:14
  154.4 28.1 %collective-permute-start.9 = (bf16[2,64,128]{2,1,0:T(8,128)(2,1)}, bf16[2,64,128]{2,1,0:T(8,128)(2,1)}, u32[]{:S(2)}, u32[]{:S(2)}) collective-permute-start(bf16[2,64,128]{2,1,0:T(8,128)(2,1)} %gather_fusion.13), channel_id=1, source_target_pairs={{2,0},{4,2},{6,4},{8,6},{10,8},{12,10},{14,12},{0,14},{3,1},{5,3},... | collective-permute-start | bytes 98312 | tf_op jit(solution)/shard_map/ppermute | solution.py:14
  156.2 31.5 %collective-permute-start.10 = (bf16[2,64,128]{2,1,0:T(8,128)(2,1)}, bf16[2,64,128]{2,1,0:T(8,128)(2,1)}, u32[]{:S(2)}, u32[]{:S(2)}) collective-permute-start(bf16[2,64,128]{2,1,0:T(8,128)(2,1)} %gather_fusion.14), channel_id=1, source_target_pairs={{12,0},{14,2},{0,4},{2,6},{4,8},{6,10},{8,12},{10,14},{13,1},{15,3... | collective-permute-start | bytes 98312 | tf_op jit(solution)/shard_map/ppermute | solution.py:14
  156.2 32.9 %collective-permute-start.11 = (bf16[2,64,128]{2,1,0:T(8,128)(2,1)}, bf16[2,64,128]{2,1,0:T(8,128)(2,1)}, u32[]{:S(2)}, u32[]{:S(2)}) collective-permute-start(bf16[2,64,128]{2,1,0:T(8,128)(2,1)} %gather_fusion.15), channel_id=1, source_target_pairs={{4,0},{6,2},{8,4},{10,6},{12,8},{14,10},{0,12},{2,14},{5,1},{7,3},... | collective-permute-start | bytes 98312 | tf_op jit(solution)/shard_map/ppermute | solution.py:14
  169.0 31.2 %collective-permute-start.16 = (f32[2,64,128]{2,1,0:T(8,128)}, f32[2,64,128]{2,1,0:T(8,128)}, u32[]{:S(2)}, u32[]{:S(2)}) collective-permute-start(f32[2,64,128]{2,1,0:T(8,128)} %get-tuple-element.73), channel_id=1, source_target_pairs={{2,0},{4,2},{6,4},{8,6},{10,8},{12,10},{14,12},{0,14},{3,1},{5,3},... | collective-permute-start | bytes 196616 | tf_op jit(solution)/shard_map/ppermute | solution.py:14
  181.1 20.5 %collective-permute-start.17 = (f32[2,64,128]{2,1,0:T(8,128)}, f32[2,64,128]{2,1,0:T(8,128)S(1)}, u32[]{:S(2)}, u32[]{:S(2)}) collective-permute-start(f32[2,64,128]{2,1,0:T(8,128)} %get-tuple-element.72), channel_id=1, source_target_pairs={{14,0},{0,2},{2,4},{4,6},{6,8},{8,10},{10,12},{12,14},{15,1},{1,3}... | collective-permute-start | bytes 196616 | tf_op jit(solution)/shard_map/ppermute | solution.py:14
  182.5 19.8 %collective-permute-start.18 = (f32[2,64,128]{2,1,0:T(8,128)}, f32[2,64,128]{2,1,0:T(8,128)S(1)}, u32[]{:S(2)}, u32[]{:S(2)}) collective-permute-start(f32[2,64,128]{2,1,0:T(8,128)} %get-tuple-element.71), channel_id=1, source_target_pairs={{4,0},{6,2},{8,4},{10,6},{12,8},{14,10},{0,12},{2,14},{5,1},{7,3},... | collective-permute-start | bytes 196616 | tf_op jit(solution)/shard_map/ppermute | solution.py:14
  187.7 15.2 %collective-permute-start.19 = (f32[2,64,128]{2,1,0:T(8,128)}, f32[2,64,128]{2,1,0:T(8,128)S(1)}, u32[]{:S(2)}, u32[]{:S(2)}) collective-permute-start(f32[2,64,128]{2,1,0:T(8,128)} %get-tuple-element.70), channel_id=1, source_target_pairs={{12,0},{14,2},{0,4},{2,6},{4,8},{6,10},{8,12},{10,14},{13,1},{15,3... | collective-permute-start | bytes 196616 | tf_op jit(solution)/shard_map/ppermute | solution.py:14
  198.1 98.6 %all-reduce.5.cloned.1.call-start = ((), (), s32[]{:S(2)}) async-start(), calls=%async_computation.1 | async-start | bytes 262144 | tf_op jit(solution)/shard_map/psum | solution.py:127
  213.4 9.1 %collective-permute-start.20 = (f32[2,64,128]{2,1,0:T(8,128)}, f32[2,64,128]{2,1,0:T(8,128)}, u32[]{:S(2)}, u32[]{:S(2)}) collective-permute-start(f32[2,64,128]{2,1,0:T(8,128)} %get-tuple-element.69), channel_id=1, source_target_pairs={{2,0},{4,2},{6,4},{8,6},{10,8},{12,10},{14,12},{0,14},{3,1},{5,3},... | collective-permute-start | bytes 196616 | tf_op jit(solution)/shard_map/ppermute | solution.py:14
  216.3 8.2 %collective-permute-start.21 = (f32[2,64,128]{2,1,0:T(8,128)}, f32[2,64,128]{2,1,0:T(8,128)}, u32[]{:S(2)}, u32[]{:S(2)}) collective-permute-start(f32[2,64,128]{2,1,0:T(8,128)} %get-tuple-element.68), channel_id=1, source_target_pairs={{14,0},{0,2},{2,4},{4,6},{6,8},{8,10},{10,12},{12,14},{15,1},{1,3}... | collective-permute-start | bytes 196616 | tf_op jit(solution)/shard_map/ppermute | solution.py:14
  216.3 10.3 %collective-permute-start.22 = (f32[2,64,128]{2,1,0:T(8,128)}, f32[2,64,128]{2,1,0:T(8,128)}, u32[]{:S(2)}, u32[]{:S(2)}) collective-permute-start(f32[2,64,128]{2,1,0:T(8,128)} %get-tuple-element.67), channel_id=1, source_target_pairs={{4,0},{6,2},{8,4},{10,6},{12,8},{14,10},{0,12},{2,14},{5,1},{7,3},... | collective-permute-start | bytes 196616 | tf_op jit(solution)/shard_map/ppermute | solution.py:14
  220.1 8.7 %collective-permute-start.23 = (f32[2,64,128]{2,1,0:T(8,128)}, f32[2,64,128]{2,1,0:T(8,128)}, u32[]{:S(2)}, u32[]{:S(2)}) collective-permute-start(f32[2,64,128]{2,1,0:T(8,128)} %get-tuple-element.66), channel_id=1, source_target_pairs={{12,0},{14,2},{0,4},{2,6},{4,8},{6,10},{8,12},{10,14},{13,1},{15,3... | collective-permute-start | bytes 196616 | tf_op jit(solution)/shard_map/ppermute | solution.py:14
  (78 other events, 664.4 us)
Sparse Core Ops, SparseCore 0:
  198.3 21.2 all-reduce.2
  222.9 73.7 all-reduce.4
